TPU v7x, 256 devices: a whole 4x4x8 slice. The times are simulated.
256 devices in a mesh: seq: 32 (over x, y, core), head: 8 (over z).
Axes of the slice: x: 4, y: 4, z: 8, core: 2. Of those that a mesh axis runs over, the one named last changes fastest.
Arguments:
- queries: bfloat16 [32768, 1024], P('seq', 'head'), may hold values from -6 to 6
- values: bfloat16 [32768, 1024], P('seq', 'head'), may hold values from -6 to 6
- w_out: bfloat16 [1024, 1024], P('head'), may hold values from -0.1875 to 0.1875
- out_grad: bfloat16 [32768, 1024], P('seq', 'head'), may hold values from -6 to 6
- slots: int32 [2, 16, 32768], P(None, 'head', 'seq'), may hold values from 0 to 32767, as said below
Outputs:
- output: bfloat16 [32768, 1024], P('seq', 'head')
- query_grad: bfloat16 [32768, 1024], P('seq', 'head')
- value_grad: bfloat16 [32768, 1024], P('seq', 'head')
- w_out_grad: float32 [1024, 1024], P('head')
Inputs may be any that keep to these rules, and one draw needn't show every extreme that they name: slots[r, h] is a permutation of the token positions: each token's place in round r's stable sort of head h's bucket ids. Of the 1024 tokens of one device of seq, exactly 48 have places among the 1024 places of one device of seq (possibly itself), 16 among those of the next device cyclically, and 32 among those of each other device.
All inputs are finite; a program needn't handle non-finite values.
Results may differ from a plain program's by a relative error of at most 0.024.
Values may be sent and summed in bfloat16 or wider, within the bound.
A program may use at most 64 MiB of HBM per device.

v0:
```python
import functools

import jax
import jax.numpy as jnp
from jax import lax
from jax.experimental import pallas as pl
from jax.experimental.pallas import tpu as pltpu
from jax.sharding import PartitionSpec as P

DH = 64
SPAN = 128
WIDE = 2 * DH
ROUNDS = 2
PAIR = 2
EXTRA = 16
PEERS = 4
MESH = pl.DeviceIdType.MESH
F32 = jnp.float32
BF16 = jnp.bfloat16
I32 = jnp.int32


def iota(shape, dim):
    return lax.broadcasted_iota(I32, shape, dim)


def one_hot(mask):
    return jnp.where(mask, 1.0, 0.0).astype(BF16)


def dot(a, b):
    return jnp.dot(a, b, preferred_element_type=F32)


def dot_nt(a, b):
    return lax.dot_general(a, b, (((1,), (1,)), ((), ())), preferred_element_type=F32)


def dot_tn(a, b):
    return lax.dot_general(a, b, (((0,), (0,)), ((), ())), preferred_element_type=F32)


def to_row(col):
    eye = iota((SPAN, SPAN), 0) == iota((SPAN, SPAN), 1)
    return jnp.sum(jnp.where(eye, col, 0.0), axis=0, keepdims=True)


def swap_halves(x):
    return pltpu.roll(x, DH, 1)


def split3(x):
    top = x.astype(BF16).astype(F32)
    rest = x - top
    middle = rest.astype(BF16).astype(F32)
    return [top, middle, rest - middle]


def kernel(
    n, z,
    q_ref, v_ref, w_ref, g_ref, slots_ref,
    out_ref, dq_ref, dv_ref, dw_ref,
    send1, recv1, send2, recv2, send3, recv3, send4, recv4,
    xqv, comb_row, comb_col, slot_row, slot_col, place_col, dest_row, place_row,
    ext, keys, inv_col, probs, log_row, outs, back, attn, attn_t, grads, delta_row,
    sorted_grad, delta_col, query_part, key_value, final, spill_out, spill_in, own_grads,
    full_grad, terms, up_in, down_in, wsend, wrecv, wsum, wall,
    ssem, rsem, bsend, brecv, psend, precv, gus, gur, gds, gdr, rus, rur, rds, rdr, wss, wrs,
):
    rows = q_ref.shape[0]
    share = rows // n
    cap = share * 3 // 2
    total = n * cap
    log_rows = rows.bit_length() - 1
    nb = rows // SPAN
    up_steps = z // 2
    down_steps = z - 1 - up_steps
    tiles = n // PEERS
    tile = PEERS * cap
    me = lax.axis_index("seq")
    me_h = lax.axis_index("head")
    up, down = lax.rem(me_h + 1, z), lax.rem(me_h + z - 1, z)
    after, before = lax.rem(me + 1, n), lax.rem(me + n - 1, n)

    barrier = pltpu.get_barrier_semaphore()

    def greet(off, carry):
        pl.semaphore_signal(barrier, inc=1, device_id={"seq": lax.rem(me + off, n)}, device_id_type=MESH)
        return carry

    lax.fori_loop(1, n, greet, 0)
    pl.semaphore_signal(barrier, inc=1, device_id={"head": up}, device_id_type=MESH)
    pl.semaphore_signal(barrier, inc=1, device_id={"head": down}, device_id_type=MESH)

    def exchange_start(send, recv, send_sem, recv_sem):
        def one(off, carry):
            peer = lax.rem(me + off, n)
            pltpu.make_async_remote_copy(
                send.at[peer], recv.at[me], send_sem, recv_sem, device_id={"seq": peer}, device_id_type=MESH
            ).start()
            return carry

        pltpu.make_async_copy(send.at[me], recv.at[me], recv_sem).start()
        lax.fori_loop(1, n, one, 0)

    def exchange_wait(recv, recv_sem):
        pltpu.make_async_copy(recv, recv, recv_sem).wait()

    def exchange_drain(send, send_sem):
        part = send.at[pl.ds(0, n - 1)]
        pltpu.make_async_copy(part, part, send_sem).wait()

    def gather_copy(going_up, step):
        if going_up:
            slot, sems, peer = lax.rem(me_h - (step - 1) + z, z), (gus, gur), up
        else:
            slot, sems, peer = lax.rem(me_h + (step - 1), z), (gds, gdr), down
        return pltpu.make_async_remote_copy(
            full_grad.at[slot], full_grad.at[slot], sems[0].at[step - 1], sems[1].at[step - 1],
            device_id={"head": peer}, device_id_type=MESH,
        )

    def gather_wait(going_up, step):
        slot = lax.rem(me_h - step + z, z) if going_up else lax.rem(me_h + step, z)
        sem = (gur if going_up else gdr).at[step - 1]
        pltpu.make_async_copy(full_grad.at[slot], full_grad.at[slot], sem).wait()

    def gather_step(step):
        for going_up, steps in ((True, up_steps), (False, down_steps)):
            if 1 < step <= steps + 1:
                gather_wait(going_up, step - 1)
            if step <= steps:
                gather_copy(going_up, step).start()

    def messages(comps, base):
        sub = iota((n, EXTRA, WIDE), 1)
        value = jnp.zeros((n, EXTRA, WIDE), F32)
        for at in range(comps):
            value = jnp.where(sub == at, base[at * n : (at + 1) * n][:, None, :], value)
        return value.astype(BF16)

    def message_parts(ref_value, comps):
        sub = iota((n, EXTRA, WIDE), 1)
        value = ref_value.astype(F32)
        return [jnp.sum(jnp.where(sub == at, value, 0.0), axis=1) for at in range(comps)]

    def scatter_small(parts, turn, target, spot):
        hot = jnp.where(iota((n, rows), 0) == target, 1.0, 0.0)
        left = jnp.concatenate([hot * part for part in parts], axis=0).astype(BF16)
        right = one_hot(iota((WIDE, rows), 0) == spot + DH * turn)
        return dot_nt(left, right)

    def gather_small(parts, turn, target, spot):
        hot = one_hot(iota((SPAN, n), 1) == target)
        wide = dot(hot, parts)
        value = wide[:, :WIDE] + wide[:, WIDE : 2 * WIDE] + wide[:, 2 * WIDE :]
        chosen = iota((SPAN, WIDE), 1) == spot + DH * turn
        return jnp.sum(jnp.where(chosen, value, 0.0), axis=1, keepdims=True)

    low_half = iota((SPAN, WIDE), 1) < DH

    for head in range(PAIR):
        for at in range(nb):
            sl = pl.ds(at * SPAN, SPAN)
            query = q_ref[sl, :].astype(F32)
            value = v_ref[sl, :].astype(F32)
            if head == 0:
                xqv[head, sl, :] = jnp.where(low_half, query, swap_halves(value)).astype(BF16)
            else:
                xqv[head, sl, :] = jnp.where(low_half, swap_halves(query), value).astype(BF16)
    full_grad[me_h] = g_ref[...]

    hots = []
    for head in range(PAIR):
        for turn in range(ROUNDS):
            slot = slots_ref[turn * PAIR + head : turn * PAIR + head + 1, :]
            hots.append(jnp.where(iota((n, rows), 0) == (slot >> log_rows), 1.0, 0.0))
    hot = jnp.concatenate(hots, axis=0)
    ahead = one_hot(iota((SPAN, SPAN), 0) < iota((SPAN, SPAN), 1))
    carry = jnp.zeros((4 * n, 1), F32)
    ranks = [[] for _ in range(4)]
    for at in range(nb):
        part = hot[:, at * SPAN : (at + 1) * SPAN]
        count = (dot(part.astype(BF16), ahead) + carry) * part
        carry = carry + jnp.sum(part, axis=1, keepdims=True)
        for b in range(4):
            ranks[b].append(jnp.sum(count[b * n : (b + 1) * n], axis=0, keepdims=True))
    position = iota((1, rows), 1)
    for head in range(PAIR):
        base = jnp.zeros((4 * n, WIDE), F32)
        for turn in range(ROUNDS):
            b = 2 * head + turn
            slot = slots_ref[turn * PAIR + head : turn * PAIR + head + 1, :]
            target = slot >> log_rows
            rank = jnp.concatenate(ranks[b], axis=1)
            rank_int = rank.astype(I32)
            comb = target * DH + rank_int
            comb_row[b] = comb
            comb_col[b] = jnp.transpose(jnp.broadcast_to(comb.astype(F32), (8, rows)))[:, :1].astype(I32)
            place = (slot & (rows - 1)) + 1
            parts = [place >> 5, place & 31, position >> 5, position & 31]
            base = base + scatter_small([p.astype(F32) for p in parts], turn, target, rank_int)
        send1[head, :, 2 * cap : 2 * cap + EXTRA, :] = messages(4, base)

    pl.semaphore_wait(barrier, n + 1)
    gather_step(1)

    def spot_rows(b):
        comb = comb_row[b]
        return (comb >> 6) * cap + (comb & (DH - 1))

    def pack_head(head, carry):
        def pack_tile(at, inner):
            line = iota((tile, rows), 0) + at * tile
            for turn in range(ROUNDS):
                hot = one_hot(line == spot_rows(2 * head + turn))
                moved = dot(hot, xqv[head]).astype(BF16).reshape(PEERS, cap, WIDE)
                send1[head, pl.ds(at * PEERS, PEERS), turn * cap : (turn + 1) * cap, :] = moved
            return inner

        lax.fori_loop(0, tiles, pack_tile, 0)
        exchange_start(send1.at[head], recv1.at[head], ssem.at[0, head], rsem.at[0, head])
        return carry

    lax.fori_loop(0, PAIR, pack_head, 0)
    gather_step(2)

    lanes = iota((1, total), 1)
    source = jnp.floor((lanes.astype(F32) + 0.5) * (1.0 / cap)).astype(I32)
    within = lanes - source * cap

    def boundary_copies(head):
        copies = []
        for turn in range(ROUNDS):
            b = 2 * head + turn
            copies.append((ext.at[b, pl.ds(rows, SPAN)], ext.at[b, pl.ds(0, SPAN)]))
        copies.append((place_row.at[head, nb], place_row.at[head, 0]))
        return [
            pltpu.make_async_remote_copy(
                src, dst, bsend.at[head, at], brecv.at[head, at], device_id={"seq": after}, device_id_type=MESH
            )
            for at, (src, dst) in enumerate(copies)
        ]

    def sort_head(head, carry):
        exchange_wait(recv1.at[head], rsem.at[0, head])
        info = message_parts(recv1[head, :, 2 * cap : 2 * cap + EXTRA, :], 4)
        info = jnp.concatenate(info, axis=0).astype(BF16)
        for turn in range(ROUNDS):
            b = 2 * head + turn
            spread = dot(info, one_hot(iota((WIDE, total), 0) == within + DH * turn))
            mine = iota((n, total), 0) == source
            place = 32.0 * spread[:n] + spread[n : 2 * n]
            token = 32.0 * spread[2 * n : 3 * n] + spread[3 * n :]
            place = jnp.sum(jnp.where(mine, place, 0.0), axis=0, keepdims=True) - 1.0
            token = jnp.sum(jnp.where(mine, token, 0.0), axis=0, keepdims=True)
            slot_row[b] = place.astype(I32)
            slot_col[b] = jnp.transpose(jnp.broadcast_to(place, (8, total)))[:, :1].astype(I32)
            comb = (source.astype(F32) * rows + token) * DH + within.astype(F32)

            def sort_tile(at, inner):
                chosen = iota((SPAN, total), 0) + at * SPAN == slot_row[b]
                got = recv1[head, :, turn * cap : (turn + 1) * cap, :].reshape(total, WIDE)
                moved = dot(one_hot(chosen), got)
                where = jnp.sum(jnp.where(chosen, comb, 0.0), axis=1, keepdims=True)
                where_int = where.astype(I32)
                sl = pl.ds(pl.multiple_of(at * SPAN, SPAN), SPAN)
                ext_sl = pl.ds(pl.multiple_of(at * SPAN + SPAN, SPAN), SPAN)
                ext[b, ext_sl, :] = moved.astype(BF16)
                place_col[b, sl, :] = where_int
                place_row[head, at + 1, turn : turn + 1, :] = to_row((where_int >> 6).astype(F32))
                home = (where_int >> (6 + log_rows)) * DH + (where_int & (DH - 1))
                dest_row[b, :, sl] = to_row(home.astype(F32)).astype(I32)
                query = jnp.where(low_half, moved, 0.0)
                mean = jnp.sum(query * query, axis=1, keepdims=True) * (1.0 / DH)
                inverse = lax.rsqrt(mean + 1e-06)
                inv_col[b, sl, :] = inverse
                keys[b, ext_sl, :] = (query * inverse).astype(BF16)
                return inner

            lax.fori_loop(0, nb, sort_tile, 0)
        for copy in boundary_copies(head):
            copy.start()
        return carry

    lax.fori_loop(0, PAIR, sort_head, 0)
    gather_step(3)

    own_token = iota((SPAN, 2 * SPAN), 1) == iota((SPAN, 2 * SPAN), 0) + SPAN

    def send_home(head, send, blocks, sums):
        def home_tile(at, inner):
            line = iota((tile, rows), 1)
            sl = pl.ds(pl.multiple_of(at * tile, EXTRA), tile)
            moved = [dot(one_hot(slot_col[2 * head + turn, sl, :] == line), blocks[2 * head + turn]) for turn in range(ROUNDS)]
            peers = pl.ds(at * PEERS, PEERS)
            if sums:
                send[head, peers, 0:cap, :] = (moved[0] + moved[1]).astype(BF16).reshape(PEERS, cap, WIDE)
            else:
                for turn in range(ROUNDS):
                    send[head, peers, turn * cap : (turn + 1) * cap, :] = (
                        moved[turn].astype(BF16).reshape(PEERS, cap, WIDE)
                    )
            return inner

        lax.fori_loop(0, tiles, home_tile, 0)

    def attend_head(head, carry):
        for copy in boundary_copies(head):
            copy.wait_recv()
        for turn in range(ROUNDS):
            b = 2 * head + turn
            query = jnp.where(low_half, ext[b, 0:SPAN, :].astype(F32), 0.0)
            mean = jnp.sum(query * query, axis=1, keepdims=True) * (1.0 / DH)
            keys[b, 0:SPAN, :] = (query * lax.rsqrt(mean + 1e-06)).astype(BF16)

        def attend_block(at, inner):
            first = pl.multiple_of(at * SPAN, SPAN)
            for turn in range(ROUNDS):
                b = 2 * head + turn
                window = ext[b, pl.ds(first, 2 * SPAN), :]
                query = ext[b, pl.ds(first + SPAN, SPAN), :]
                scores = dot_nt(query, keys[b, pl.ds(first, 2 * SPAN), :]) * (DH ** (-0.5))
                places = jnp.concatenate(
                    [place_row[head, at, turn : turn + 1, :], place_row[head, at + 1, turn : turn + 1, :]], axis=1
                )
                own_place = (place_col[b, pl.ds(first, SPAN), :] >> 6).astype(F32)
                scores = scores - jnp.where(own_token, 100000.0, 0.0)
                scores = scores - jnp.where(places > own_place, 1000000000.0, 0.0)
                top = jnp.max(scores, axis=1, keepdims=True)
                weight = jnp.exp(scores - top)
                norm = jnp.sum(weight, axis=1, keepdims=True)
                prob = (weight * (1.0 / norm)).astype(BF16)
                probs[b, pl.ds(first, SPAN), :] = prob
                log_row[b, :, pl.ds(first, SPAN)] = to_row(top + jnp.log(norm))
                result = dot(prob, window)
                if turn == 0:
                    result = swap_halves(result)
                result = jnp.where(low_half == (turn == 0), result, 0.0)
                outs[b, pl.ds(first, SPAN), :] = result.astype(BF16)
            return inner

        lax.fori_loop(0, nb, attend_block, 0)
        base = jnp.zeros((3 * n, WIDE), F32)
        for turn in range(ROUNDS):
            b = 2 * head + turn
            dest = dest_row[b]
            base = base + scatter_small(split3(log_row[b]), turn, dest >> 6, dest & (DH - 1))
        send2[head, :, cap : cap + EXTRA, :] = messages(3, base)
        send_home(head, send2, outs, True)
        exchange_start(send2.at[head], recv2.at[head], ssem.at[1, head], rsem.at[1, head])
        return carry

    lax.fori_loop(0, PAIR, attend_head, 0)
    for step in range(4, up_steps + 2):
        gather_step(step)
    for step in range(min(3, up_steps) + 1, 4):
        gather_step(step)

    def back_tile(at, carry):
        sl = pl.ds(pl.multiple_of(at * SPAN, SPAN), SPAN)
        value = jnp.zeros((SPAN, WIDE), F32)
        for chunk in range(z):
            value = value + dot_nt(full_grad[chunk, sl, :], w_ref[:, chunk * WIDE : (chunk + 1) * WIDE])
        value = value.astype(BF16).astype(F32)
        other = swap_halves(value)
        back[0, sl, :] = jnp.where(low_half, value, other)
        back[1, sl, :] = jnp.where(low_half, other, value)
        return carry

    lax.fori_loop(0, nb, back_tile, 0)

    def combine_head(head, carry):
        exchange_wait(recv2.at[head], rsem.at[1, head])
        parts = jnp.concatenate(
            message_parts(recv2[head, :, cap : cap + EXTRA, :], 3), axis=1
        ).astype(BF16)

        def combine_tile(at, inner):
            sl = pl.ds(pl.multiple_of(at * SPAN, SPAN), SPAN)
            got = recv2[head, :, 0:cap, :].reshape(total, WIDE)
            logs, moved = [], []
            for turn in range(ROUNDS):
                comb = comb_col[2 * head + turn, sl, :]
                target, spot = comb >> 6, comb & (DH - 1)
                logs.append(gather_small(parts, turn, target, spot))
                moved.append(dot(one_hot(iota((SPAN, total), 1) == target * cap + spot), got))
            top = jnp.maximum(logs[0], logs[1])
            raised = [jnp.exp(log - top) for log in logs]
            whole = raised[0] + raised[1]
            mixing = [r / whole for r in raised]
            mix = jnp.where(low_half, mixing[0], mixing[1])
            product = jnp.where(low_half, moved[0], moved[1]) * mix
            combined = product + swap_halves(product)
            attn[head, sl, :] = combined.astype(BF16)
            grad = back[head, sl, :]
            inside = 0.5 * jnp.sum(grad * combined, axis=1, keepdims=True)
            sent = grad * mix
            for turn in range(ROUNDS):
                b = 2 * head + turn
                grads[b, sl, :] = jnp.where(low_half == (turn == 0), sent, 0.0).astype(BF16)
                delta_row[b, :, sl] = to_row(mixing[turn] * inside)
            return inner

        lax.fori_loop(0, nb, combine_tile, 0)
        base = jnp.zeros((3 * n, WIDE), F32)
        for turn in range(ROUNDS):
            b = 2 * head + turn
            comb = comb_row[b]
            base = base + scatter_small(split3(delta_row[b]), turn, comb >> 6, comb & (DH - 1))
        send3[head, :, cap : cap + EXTRA, :] = messages(3, base)

        def pack_tile(at, inner):
            line = iota((tile, rows), 0) + at * tile
            moved = [dot(one_hot(line == spot_rows(2 * head + turn)), grads[2 * head + turn]) for turn in range(ROUNDS)]
            send3[head, pl.ds(at * PEERS, PEERS), 0:cap, :] = (
                (moved[0] + moved[1]).astype(BF16).reshape(PEERS, cap, WIDE)
            )
            return inner

        lax.fori_loop(0, tiles, pack_tile, 0)
        exchange_start(send3.at[head], recv3.at[head], ssem.at[2, head], rsem.at[2, head])
        return carry

    lax.fori_loop(0, PAIR, combine_head, 0)

    def term_tile(at, carry):
        sl = pl.ds(pl.multiple_of(at * SPAN, SPAN), SPAN)
        both = jnp.where(low_half, attn[0, sl, :].astype(F32), attn[1, sl, :].astype(F32))
        attn_t[:, sl] = jnp.transpose(both).astype(BF16)
        result = dot(both.astype(BF16), w_ref[...]).astype(BF16)
        for chunk in range(z):
            terms[chunk, sl, :] = result[:, chunk * WIDE : (chunk + 1) * WIDE]
        return carry

    lax.fori_loop(0, nb, term_tile, 0)

    def reduce_copy(going_up, step, first):
        sems = (rus, rur) if going_up else (rds, rdr)
        steps = up_steps if going_up else down_steps
        box = up_in if going_up else down_in
        if first:
            slot = lax.rem(me_h + steps, z) if going_up else lax.rem(me_h - steps + z, z)
            src = terms.at[slot]
        else:
            src = box.at[step - 2]
        return pltpu.make_async_remote_copy(
            src, box.at[step - 1], sems[0].at[step - 1], sems[1].at[step - 1],
            device_id={"head": up if going_up else down}, device_id_type=MESH,
        )

    def reduce_wait(going_up, step):
        box, sem = (up_in, rur) if going_up else (down_in, rdr)
        pltpu.make_async_copy(box.at[step - 1], box.at[step - 1], sem.at[step - 1]).wait()

    def reduce_step(step, ways):
        for going_up in ways:
            steps = up_steps if going_up else down_steps
            reduce_wait(going_up, step - 1)
            gone = steps - step + 1
            slot = lax.rem(me_h + gone, z) if going_up else lax.rem(me_h - gone + z, z)
            box = up_in if going_up else down_in
            box[step - 2] = (box[step - 2].astype(F32) + terms[slot].astype(F32)).astype(BF16)
            reduce_copy(going_up, step, False).start()

    reduce_copy(True, 1, True).start()
    if down_steps:
        reduce_copy(False, 1, True).start()

    pieces = n // z
    piece = WIDE // pieces
    for chunk in range(z):
        grad = dot(attn_t[...], full_grad[chunk]).astype(BF16)
        for at in range(pieces):
            wsend[chunk * pieces + at] = grad[at * piece : (at + 1) * piece]
    exchange_start(wsend, wrecv, wss.at[0], wrs.at[0])

    def spill_copy(head):
        return pltpu.make_async_remote_copy(
            spill_out.at[head], spill_in.at[head], psend.at[head], precv.at[head],
            device_id={"seq": before}, device_id_type=MESH,
        )

    early = up_steps >= 3 and down_steps >= 3

    def backward_head(head, carry):
        exchange_wait(recv3.at[head], rsem.at[2, head])
        parts = jnp.concatenate(
            message_parts(recv3[head, :, cap : cap + EXTRA, :], 3), axis=1
        ).astype(BF16)
        for turn in range(ROUNDS):
            b = 2 * head + turn

            def sort_tile(at, inner):
                sl = pl.ds(pl.multiple_of(at * SPAN, SPAN), SPAN)
                chosen = iota((SPAN, total), 0) + at * SPAN == slot_row[b]
                got = recv3[head, :, 0:cap, :].reshape(total, WIDE)
                moved = dot(one_hot(chosen), got)
                if turn == 0:
                    moved = swap_halves(moved)
                sorted_grad[b, sl, :] = jnp.where(low_half, 0.0, moved).astype(BF16)
                where = place_col[b, sl, :]
                delta_col[b, sl, :] = gather_small(parts, turn, where >> (6 + log_rows), where & (DH - 1))
                return inner

            lax.fori_loop(0, nb, sort_tile, 0)
            key_value[b, 0:SPAN, :] = jnp.zeros((SPAN, WIDE), F32)

        if early:
            reduce_step(head + 2, (True, False))

        def backward_block(at, inner):
            first = pl.multiple_of(at * SPAN, SPAN)
            sl = pl.ds(first, SPAN)
            nxt = pl.ds(first + SPAN, SPAN)
            for turn in range(ROUNDS):
                b = 2 * head + turn
                window = ext[b, pl.ds(first, 2 * SPAN), :]
                grad = sorted_grad[b, sl, :]
                prob = probs[b, sl, :]
                slope = prob.astype(F32) * (dot_nt(grad, window) - delta_col[b, sl, :])
                slope = slope.astype(BF16)
                query_part[b, sl, :] = dot(slope, keys[b, pl.ds(first, 2 * SPAN), :])
                query = jnp.where(low_half, ext[b, nxt, :].astype(F32) * (DH ** (-0.5)), 0.0).astype(BF16)
                both = dot_tn(
                    jnp.concatenate([slope, prob], axis=0), jnp.concatenate([query, grad], axis=0)
                )
                key_value[b, sl, :] += both[:SPAN]
                key_value[b, nxt, :] = both[SPAN:]

            @pl.when(at == 0)
            def _():
                for turn in range(ROUNDS):
                    spill_out[head, turn] = key_value[2 * head + turn, 0:SPAN, :].astype(BF16)
                spill_copy(head).start()

            return inner

        lax.fori_loop(0, nb, backward_block, 0)
        spill_copy(head).wait_recv()
        for turn in range(ROUNDS):
            key_value[2 * head + turn, rows : rows + SPAN, :] += spill_in[head, turn].astype(F32)

        def final_tile(at, inner):
            first = pl.multiple_of(at * SPAN, SPAN)
            sl = pl.ds(first, SPAN)
            nxt = pl.ds(first + SPAN, SPAN)
            for turn in range(ROUNDS):
                b = 2 * head + turn
                query = jnp.where(low_half, ext[b, nxt, :].astype(F32), 0.0)
                inverse = inv_col[b, sl, :]
                sums = key_value[b, nxt, :]
                mean = jnp.sum(query * sums, axis=1, keepdims=True) * (1.0 / DH)
                query_total = (
                    query_part[b, sl, :] * (DH ** (-0.5))
                    + inverse * sums
                    - query * (inverse * inverse * inverse) * mean
                )
                final[b, sl, :] = jnp.where(low_half, query_total, sums).astype(BF16)
            return inner

        lax.fori_loop(0, nb, final_tile, 0)
        send_home(head, send4, final, False)
        exchange_start(send4.at[head], recv4.at[head], ssem.at[3, head], rsem.at[3, head])
        return carry

    lax.fori_loop(0, PAIR, backward_head, 0)

    for step in range(4 if early else 2, up_steps + 1):
        reduce_step(step, (True,))
    for step in range(4 if early else 2, down_steps + 1):
        reduce_step(step, (False,))

    exchange_wait(wrecv, wrs.at[0])
    wsum[...] = jnp.broadcast_to(jnp.sum(wrecv[...].astype(F32), axis=0).astype(BF16)[None], wsum.shape)
    exchange_start(wsum, wall, wss.at[1], wrs.at[1])

    def final_head(head, carry):
        exchange_wait(recv4.at[head], rsem.at[3, head])

        def own_tile(at, inner):
            sl = pl.ds(pl.multiple_of(at * SPAN, SPAN), SPAN)
            value = jnp.zeros((SPAN, WIDE), F32)
            for turn in range(ROUNDS):
                comb = comb_col[2 * head + turn, sl, :]
                got = recv4[head, :, turn * cap : (turn + 1) * cap, :].reshape(total, WIDE)
                spot = (comb >> 6) * cap + (comb & (DH - 1))
                value = value + dot(one_hot(iota((SPAN, total), 1) == spot), got)
            own_grads[head, sl, :] = value
            return inner

        lax.fori_loop(0, nb, own_tile, 0)
        return carry

    lax.fori_loop(0, PAIR, final_head, 0)

    def output_tile(at, carry):
        sl = pl.ds(pl.multiple_of(at * SPAN, SPAN), SPAN)
        first, second = own_grads[0, sl, :], own_grads[1, sl, :]
        dq_ref[sl, :] = jnp.where(low_half, first, swap_halves(second)).astype(BF16)
        dv_ref[sl, :] = jnp.where(low_half, swap_halves(first), second).astype(BF16)
        return carry

    lax.fori_loop(0, nb, output_tile, 0)

    reduce_wait(True, up_steps)
    if down_steps:
        reduce_wait(False, down_steps)

    def result_tile(at, carry):
        sl = pl.ds(pl.multiple_of(at * SPAN, SPAN), SPAN)
        value = terms[me_h, sl, :].astype(F32) + up_in[up_steps - 1, sl, :].astype(F32)
        if down_steps:
            value = value + down_in[down_steps - 1, sl, :].astype(F32)
        out_ref[sl, :] = value.astype(BF16)
        return carry

    lax.fori_loop(0, nb, result_tile, 0)

    exchange_wait(wall, wrs.at[1])
    for chunk in range(z):
        for at in range(pieces):
            value = wall[chunk * pieces + at].astype(F32) * (n * rows) ** (-0.5)
            dw_ref[at * piece : (at + 1) * piece, chunk * WIDE : (chunk + 1) * WIDE] = value

    for head in range(PAIR):
        for at, send in enumerate((send1, send2, send3, send4)):
            exchange_drain(send.at[head], ssem.at[at, head])
        for copy in boundary_copies(head):
            copy.wait_send()
        spill_copy(head).wait_send()
    exchange_drain(wsend, wss.at[0])
    exchange_drain(wsum, wss.at[1])
    for going_up, steps in ((True, up_steps), (False, down_steps)):
        for step in range(1, steps + 1):
            gather_copy(going_up, step).wait_send()
            reduce_copy(going_up, step, step == 1).wait_send()


def per_device(n, z, queries, values, w_out, out_grad, slots):
    rows = queries.shape[0]
    cap = rows // n * 3 // 2
    total = n * cap
    nb = rows // SPAN
    up_steps = z // 2
    down_steps = max(z - 1 - up_steps, 1)
    piece = WIDE * z // n
    batch = ROUNDS * PAIR
    vmem = pltpu.VMEM
    dma = pltpu.SemaphoreType.DMA
    wide1 = (PAIR, n, 2 * cap + EXTRA, WIDE)
    wide2 = (PAIR, n, cap + EXTRA, WIDE)
    wide4 = (PAIR, n, 2 * cap, WIDE)
    scratch = [
        vmem(wide1, BF16), vmem(wide1, BF16),
        vmem(wide2, BF16), vmem(wide2, BF16),
        vmem(wide2, BF16), vmem(wide2, BF16),
        vmem(wide4, BF16), vmem(wide4, BF16),
        vmem((PAIR, rows, WIDE), BF16),
        vmem((batch, 1, rows), I32),
        vmem((batch, rows, 1), I32),
        vmem((batch, 1, total), I32),
        vmem((batch, total, 1), I32),
        vmem((batch, rows, 1), I32),
        vmem((batch, 1, rows), I32),
        vmem((PAIR, nb + 1, 8, SPAN), F32),
        vmem((batch, rows + SPAN, WIDE), BF16),
        vmem((batch, rows + SPAN, WIDE), BF16),
        vmem((batch, rows, 1), F32),
        vmem((batch, rows, 2 * SPAN), BF16),
        vmem((batch, 1, rows), F32),
        vmem((batch, rows, WIDE), BF16),
        vmem((PAIR, rows, WIDE), F32),
        vmem((PAIR, rows, WIDE), BF16),
        vmem((WIDE, rows), BF16),
        vmem((batch, rows, WIDE), BF16),
        vmem((batch, 1, rows), F32),
        vmem((batch, rows, WIDE), BF16),
        vmem((batch, rows, 1), F32),
        vmem((batch, rows, WIDE), F32),
        vmem((batch, rows + SPAN, WIDE), F32),
        vmem((batch, rows, WIDE), BF16),
        vmem((PAIR, ROUNDS, SPAN, WIDE), BF16),
        vmem((PAIR, ROUNDS, SPAN, WIDE), BF16),
        vmem((PAIR, rows, WIDE), F32),
        vmem((z, rows, WIDE), BF16),
        vmem((z, rows, WIDE), BF16),
        vmem((up_steps, rows, WIDE), BF16),
        vmem((down_steps, rows, WIDE), BF16),
        vmem((n, piece, WIDE), BF16),
        vmem((n, piece, WIDE), BF16),
        vmem((n, piece, WIDE), BF16),
        vmem((n, piece, WIDE), BF16),
        dma((4, PAIR)), dma((4, PAIR)),
        dma((PAIR, 3)), dma((PAIR, 3)),
        dma((PAIR,)), dma((PAIR,)),
        dma((up_steps,)), dma((up_steps,)), dma((down_steps,)), dma((down_steps,)),
        dma((up_steps,)), dma((up_steps,)), dma((down_steps,)), dma((down_steps,)),
        dma((2,)), dma((2,)),
    ]
    local = pl.BlockSpec(memory_space=pltpu.VMEM)
    return pl.pallas_call(
        functools.partial(kernel, n, z),
        out_shape=(
            jax.ShapeDtypeStruct((rows, WIDE), BF16),
            jax.ShapeDtypeStruct((rows, WIDE), BF16),
            jax.ShapeDtypeStruct((rows, WIDE), BF16),
            jax.ShapeDtypeStruct((WIDE, z * WIDE), F32),
        ),
        in_specs=[local] * 5,
        out_specs=[local] * 4,
        scratch_shapes=scratch,
        compiler_params=pltpu.CompilerParams(
            collective_id=0, has_side_effects=True, vmem_limit_bytes=62 * 1024 * 1024
        ),
    )(queries, values, w_out, out_grad, slots.reshape(batch, rows))


def solution(mesh):
    placed = (
        P("seq", "head"),
        P("seq", "head"),
        P("head", None),
        P("seq", "head"),
        P(None, "head", "seq"),
    )
    return jax.shard_map(
        functools.partial(per_device, mesh.shape["seq"], mesh.shape["head"]),
        mesh=mesh,
        in_specs=placed,
        out_specs=(P("seq", "head"), P("seq", "head"), P("seq", "head"), P("head", None)),
        check_vma=False,
    )
```

profile of v0, /device:TPU:1, one launch (start us, length us, event | category | flops | bytes accessed | tf_op | source)
XLA Modules:
  0.0 161.3 jit_solution(4065689496290713226)
XLA Ops:
  0.6 1.3 reshape.11.slots_ref
  2.0 155.3 %shard_map.84 = (bf16[1024,128]{1,0:T(8,128)(2,1)}, bf16[1024,128]{1,0:T(8,128)(2,1)}, bf16[1024,128]{1,0:T(8,128)(2,1)}, f32[128,1024]{1,0:T(8,128)}) custom-call(bf16[1024,128]{1,0:T(8,128)(2,1)} %q_ref.1, bf16[1024,128]{1,0:T(8,128)(2,1)} %v_ref.1, bf16[128,1024]{1,0:T(8,128)(2,1)} %w_ref.1, bf16[1024,128]{1,0:T(8,128)(2,1)} %g_ref.1, ...), custom_call_target="tpu_custom_call" | custom-call | tf_op jit(solution)/shard_map/pallas_call | solution.py:702
  157.3 0.0 copy-start.2
  157.3 0.0 copy-start.1
  157.3 1.7 %copy.13 = bf16[1024,128]{1,0:T(8,128)(2,1)} copy(bf16[1024,128]{1,0:T(8,128)(2,1)} %get-tuple-element.8) | data formatting | bytes 524288
  159.1 0.0 copy-done.2
  159.1 0.0 copy-start
  159.1 0.7 copy.14
  159.8 0.0 copy-done.1
  159.8 0.7 copy.15
  160.5 0.0 copy-done
  160.5 0.8 copy.16
Async XLA Ops:
  157.3 1.7 %copy-start.2 = (bf16[1024,128]{1,0:T(8,128)(2,1)S(1)}, bf16[1024,128]{1,0:T(8,128)(2,1)}, u32[]{:S(2)}) copy-start(bf16[1024,128]{1,0:T(8,128)(2,1)} %get-tuple-element.9) | copy-start | bytes 786436
  157.3 2.4 %copy-start.1 = (bf16[1024,128]{1,0:T(8,128)(2,1)S(1)}, bf16[1024,128]{1,0:T(8,128)(2,1)}, u32[]{:S(2)}) copy-start(bf16[1024,128]{1,0:T(8,128)(2,1)} %get-tuple-element.10) | copy-start | bytes 786436
  159.1 1.4 copy-start
where the time goes:
time: 161 us
  Pallas kernels  155 us (96%)
  local copies, waits for them, and re-layouts  5.28 us (3%)
    pallas_call x1, Pallas kernels, per_device(): pl.pallas_call(functools.partial(kernel, n, z), out_shape=(jax.ShapeDtype...  155 us
    unnamed x10, local copies, waits for them, and re-layouts  3.94 us

commit v1 on v0

--- a/solution.py
+++ b/solution.py
@@ -18,6 +18,8 @@
 F32 = jnp.float32
 BF16 = jnp.bfloat16
 I32 = jnp.int32
+I16 = jnp.int16
+PACK = 16
 
 
 def iota(shape, dim):
@@ -26,6 +28,25 @@
 
 def one_hot(mask):
     return jnp.where(mask, 1.0, 0.0).astype(BF16)
+
+
+def select16(masks, axis):
+    one, zero = jnp.ones((), BF16), jnp.zeros((), BF16)
+    return jnp.concatenate([jnp.where(mask, one, zero) for mask in masks], axis=axis)
+
+
+def hot_rows(row, start, count):
+    wide = (PACK, row.shape[1])
+    near = jnp.broadcast_to(row - start, wide).astype(I16)
+    line = iota(wide, 0).astype(I16)
+    return select16([near == line + jnp.int16(at) for at in range(0, count, PACK)], 0)
+
+
+def hot_cols(col, count):
+    wide = (col.shape[0], SPAN)
+    near = jnp.broadcast_to(col, wide).astype(I16)
+    line = iota(wide, 1).astype(I16)
+    return select16([near == line + jnp.int16(at) for at in range(0, count, SPAN)], 1)
 
 
 def dot(a, b):
@@ -211,9 +232,8 @@
 
     def pack_head(head, carry):
         def pack_tile(at, inner):
-            line = iota((tile, rows), 0) + at * tile
             for turn in range(ROUNDS):
-                hot = one_hot(line == spot_rows(2 * head + turn))
+                hot = hot_rows(spot_rows(2 * head + turn), at * tile, tile)
                 moved = dot(hot, xqv[head]).astype(BF16).reshape(PEERS, cap, WIDE)
                 send1[head, pl.ds(at * PEERS, PEERS), turn * cap : (turn + 1) * cap, :] = moved
             return inner
@@ -290,9 +310,8 @@
 
     def send_home(head, send, blocks, sums):
         def home_tile(at, inner):
-            line = iota((tile, rows), 1)
             sl = pl.ds(pl.multiple_of(at * tile, EXTRA), tile)
-            moved = [dot(one_hot(slot_col[2 * head + turn, sl, :] == line), blocks[2 * head + turn]) for turn in range(ROUNDS)]
+            moved = [dot(hot_cols(slot_col[2 * head + turn, sl, :], rows), blocks[2 * head + turn]) for turn in range(ROUNDS)]
             peers = pl.ds(at * PEERS, PEERS)
             if sums:
                 send[head, peers, 0:cap, :] = (moved[0] + moved[1]).astype(BF16).reshape(PEERS, cap, WIDE)
@@ -384,7 +403,7 @@
                 comb = comb_col[2 * head + turn, sl, :]
                 target, spot = comb >> 6, comb & (DH - 1)
                 logs.append(gather_small(parts, turn, target, spot))
-                moved.append(dot(one_hot(iota((SPAN, total), 1) == target * cap + spot), got))
+                moved.append(dot(hot_cols(target * cap + spot, total), got))
             top = jnp.maximum(logs[0], logs[1])
             raised = [jnp.exp(log - top) for log in logs]
             whole = raised[0] + raised[1]
@@ -411,8 +430,10 @@
         send3[head, :, cap : cap + EXTRA, :] = messages(3, base)
 
         def pack_tile(at, inner):
-            line = iota((tile, rows), 0) + at * tile
-            moved = [dot(one_hot(line == spot_rows(2 * head + turn)), grads[2 * head + turn]) for turn in range(ROUNDS)]
+            moved = [
+                dot(hot_rows(spot_rows(2 * head + turn), at * tile, tile), grads[2 * head + turn])
+                for turn in range(ROUNDS)
+            ]
             send3[head, pl.ds(at * PEERS, PEERS), 0:cap, :] = (
                 (moved[0] + moved[1]).astype(BF16).reshape(PEERS, cap, WIDE)
             )
@@ -493,9 +514,8 @@
 
             def sort_tile(at, inner):
                 sl = pl.ds(pl.multiple_of(at * SPAN, SPAN), SPAN)
-                chosen = iota((SPAN, total), 0) + at * SPAN == slot_row[b]
                 got = recv3[head, :, 0:cap, :].reshape(total, WIDE)
-                moved = dot(one_hot(chosen), got)
+                moved = dot(hot_rows(slot_row[b], at * SPAN, SPAN), got)
                 if turn == 0:
                     moved = swap_halves(moved)
                 sorted_grad[b, sl, :] = jnp.where(low_half, 0.0, moved).astype(BF16)
@@ -585,7 +605,7 @@
                 comb = comb_col[2 * head + turn, sl, :]
                 got = recv4[head, :, turn * cap : (turn + 1) * cap, :].reshape(total, WIDE)
                 spot = (comb >> 6) * cap + (comb & (DH - 1))
-                value = value + dot(one_hot(iota((SPAN, total), 1) == spot), got)
+                value = value + dot(hot_cols(spot, total), got)
             own_grads[head, sl, :] = value
             return inner
 

time: 161 us -> 158 us (0.981)
  Pallas kernels: 155 us -> 152 us
    pallas_call x1, Pallas kernels: 155 us -> 152 us  [per_device(): pl.pallas_call(functools.partial(kernel, n, z), out_shape=(jax.ShapeDtype...]
where the time goes in v1:
time: 158 us
  Pallas kernels  152 us (96%)
  local copies, waits for them, and re-layouts  5.28 us (3%)
    pallas_call x1, Pallas kernels, per_device(): pl.pallas_call(functools.partial(kernel, n, z), out_shape=(jax.ShapeDtype...  152 us
    unnamed x10, local copies, waits for them, and re-layouts  3.94 us

profile of v1, /device:TPU:1, one launch (start us, length us, event | category | flops | bytes accessed | tf_op | source)
XLA Modules:
  0.0 157.6 jit_solution(9434917000775794457)
XLA Ops:
  0.6 1.3 reshape.11.slots_ref
  2.0 151.7 %shard_map.84 = (bf16[1024,128]{1,0:T(8,128)(2,1)}, bf16[1024,128]{1,0:T(8,128)(2,1)}, bf16[1024,128]{1,0:T(8,128)(2,1)}, f32[128,1024]{1,0:T(8,128)}) custom-call(bf16[1024,128]{1,0:T(8,128)(2,1)} %q_ref.1, bf16[1024,128]{1,0:T(8,128)(2,1)} %v_ref.1, bf16[128,1024]{1,0:T(8,128)(2,1)} %w_ref.1, bf16[1024,128]{1,0:T(8,128)(2,1)} %g_ref.1, ...), custom_call_target="tpu_custom_call" | custom-call | tf_op jit(solution)/shard_map/pallas_call | solution.py:722
  153.6 0.0 copy-start.2
  153.6 0.0 copy-start.1
  153.7 1.7 %copy.13 = bf16[1024,128]{1,0:T(8,128)(2,1)} copy(bf16[1024,128]{1,0:T(8,128)(2,1)} %get-tuple-element.8) | data formatting | bytes 524288
  155.4 0.0 copy-done.2
  155.4 0.0 copy-start
  155.4 0.7 copy.14
  156.1 0.0 copy-done.1
  156.1 0.7 copy.15
  156.8 0.0 copy-done
  156.8 0.8 copy.16
Async XLA Ops:
  153.6 1.7 %copy-start.2 = (bf16[1024,128]{1,0:T(8,128)(2,1)S(1)}, bf16[1024,128]{1,0:T(8,128)(2,1)}, u32[]{:S(2)}) copy-start(bf16[1024,128]{1,0:T(8,128)(2,1)} %get-tuple-element.9) | copy-start | bytes 786436
  153.6 2.4 %copy-start.1 = (bf16[1024,128]{1,0:T(8,128)(2,1)S(1)}, bf16[1024,128]{1,0:T(8,128)(2,1)}, u32[]{:S(2)}) copy-start(bf16[1024,128]{1,0:T(8,128)(2,1)} %get-tuple-element.10) | copy-start | bytes 786436
  155.4 1.4 copy-start
